TPU v7x, 32 devices: a whole 2x2x4 slice. The times are simulated.
32 devices in a mesh: dp: 8 (over z, y), mp: 4 (over x, core).
Axes of the slice: x: 2, y: 2, z: 4, core: 2. Of those that a mesh axis runs over, the one named last changes fastest.
Arguments:
- hidden_in: bfloat16 [16384, 2048], P('dp', 'mp'), may hold values from -18 to 18
- cotangent: bfloat16 [16384, 2048], P('dp', 'mp'), may hold values from -6 to 6
- segment_ids: int32 [16, 1024], P('dp'), may hold values from 0 to 15, never falling along the last dimension, each value on 1 to 512 neighbouring positions
- adapter_ids: int32 [16], P('dp'), may hold values from 0 to 7
- ln_gain: float32 [2048], replicated, may hold values from 0.5 to 1.5
- ln_bias: float32 [2048], replicated, may hold values from -4 to 4
- w_qkv: bfloat16 [2048, 3, 2048], P('dp', None, 'mp'), may hold values from -0.125 to 0.125
- b_qkv: bfloat16 [3, 2048], P(None, 'mp'), may hold values from -4 to 4
- w_out: bfloat16 [2048, 2048], P('mp', 'dp'), may hold values from -0.375 to 0.375
- b_out: bfloat16 [2048], P('mp'), may hold values from -4 to 4
- w_fc1: bfloat16 [2048, 8192], P('dp', 'mp'), may hold values from -0.125 to 0.125
- b_fc1: bfloat16 [8192], P('mp'), may hold values from -4 to 4
- w_fc2: bfloat16 [8192, 2048], P('mp', 'dp'), may hold values from -0.0625 to 0.0625
- b_fc2: bfloat16 [2048], P('mp'), may hold values from -4 to 4
- down_input_factors: bfloat16 [8, 4, 16, 2048], P(None, None, None, 'dp'), may hold values from -0.125 to 0.125
- up_qkv: bfloat16 [8, 16, 3, 2048], P(None, 'dp', None, 'mp'), may hold values from -1.5 to 1.5
- up_fc1: bfloat16 [8, 16, 8192], P(None, 'dp', 'mp'), may hold values from -1.5 to 1.5
- down_o: bfloat16 [8, 16, 2048], P(None, 'dp', 'mp'), may hold values from -0.375 to 0.375
- down_fc2: bfloat16 [8, 16, 8192], P(None, 'dp', 'mp'), may hold values from -0.0625 to 0.0625
- up_output_factors: bfloat16 [8, 2, 16, 2048], P(None, None, 'dp', 'mp'), may hold values from -3 to 3
Outputs:
- output: bfloat16 [16384, 2048], P('dp', 'mp')
- grad_in: bfloat16 [16384, 2048], P('dp', 'mp')
- grad_down_x: float32 [8, 4, 16, 2048], P(None, None, None, 'dp')
- grad_up_qkv: float32 [8, 16, 3, 2048], P(None, 'dp', None, 'mp')
- grad_up_fc1: float32 [8, 16, 8192], P(None, 'dp', 'mp')
- grad_down_o: float32 [8, 16, 2048], P(None, 'dp', 'mp')
- grad_down_fc2: float32 [8, 16, 8192], P(None, 'dp', 'mp')
- grad_up_out: float32 [8, 2, 16, 2048], P(None, None, 'dp', 'mp')
Inputs may be any that keep to these rules, and one draw needn't show every extreme that they name: `segment_ids`: within a sequence the ids never fall; a document is a run of equal ids.
All inputs are finite; a program needn't handle non-finite values.
Results may differ from a plain program's by a relative error of at most 0.0094.
Values may be sent and summed in bfloat16 or wider, within the bound.
No kernel may reach another device: no remote copies, remote signals or barrier semaphores. Data moves between devices by JAX's collectives and lax.ppermute only.
A program may use at most 320 MiB of HBM per device.

v0:
```python
import jax
import jax.numpy as jnp
from jax import lax
from jax.sharding import PartitionSpec as P

MODEL_WIDTH = 2048
HEAD_DIM = 64
ROT = 32
NAD = 8
LEN = 1024


EPSILON = 1e-05
GELU_C = 0.7978845608028654
SUMMATION_DTYPE = jnp.float32


def gelu_tanh(values):
    return 0.5 * values * (1.0 + jnp.tanh(GELU_C * (values + 0.044715 * values * values * values)))


def angles(segments):
    places = jnp.arange(segments.shape[1], dtype=jnp.int32)
    change = jnp.concatenate(
        [jnp.ones((segments.shape[0], 1), dtype=bool), segments[:, 1:] != segments[:, :-1]], axis=1
    )
    starts = lax.cummax(jnp.where(change, places[None, :], 0), axis=1)
    offsets = (places[None, :] - starts).astype(jnp.float32)
    inverse_freq = 10000.0 ** (-2.0 * jnp.arange(ROT // 2, dtype=jnp.float32) / ROT)
    phase = offsets[:, :, None, None] * inverse_freq
    return (jnp.cos(phase), jnp.sin(phase))


def rotate(tensor, cosine, sine, inverse):
    half_rot = ROT // 2
    first = tensor[..., :half_rot]
    second = tensor[..., half_rot:ROT]
    rest_dims = tensor[..., ROT:]
    if inverse:
        return jnp.concatenate(
            [first * cosine + second * sine, second * cosine - first * sine, rest_dims], axis=-1
        )
    return jnp.concatenate(
        [first * cosine - second * sine, second * cosine + first * sine, rest_dims], axis=-1
    )


def allowed_keys(segment):
    places = jnp.arange(segment.shape[0])
    return (places[None, :] <= places[:, None]) & (segment[None, :] == segment[:, None])


def masked_scores(queries, keys_low, segment):
    scores = jnp.einsum("qhe,khe->hqk", queries, keys_low, preferred_element_type=SUMMATION_DTYPE)
    return jnp.where(allowed_keys(segment)[None], scores, -1e30)


def attend(packed):
    queries, keys_low, values_low, segment = packed
    scores = masked_scores(queries, keys_low, segment)
    top_score = jnp.max(scores, axis=-1, keepdims=True)
    raised = jnp.exp(scores - top_score)
    totals = jnp.sum(raised, axis=-1, keepdims=True)
    prob_low = (raised / totals).astype(jnp.bfloat16)
    context = jnp.einsum(
        "hqk,khe->qhe", prob_low, values_low, preferred_element_type=SUMMATION_DTYPE
    ).astype(jnp.bfloat16)
    return (context, (top_score + jnp.log(totals))[..., 0])


def attend_back(packed):
    queries, keys_low, values_low, segment, log_total, grad_ctx = packed
    scores = masked_scores(queries, keys_low, segment)
    probs = jnp.exp(scores - log_total[..., None])
    prob_low = probs.astype(jnp.bfloat16)
    grad_prob = jnp.einsum(
        "qhe,khe->hqk", grad_ctx, values_low, preferred_element_type=SUMMATION_DTYPE
    )
    delta_row = jnp.sum(probs * grad_prob, axis=-1, keepdims=True)
    grad_score = (probs * (grad_prob - delta_row)).astype(jnp.bfloat16)
    grad_query = jnp.einsum(
        "hqk,khe->qhe", grad_score, keys_low, preferred_element_type=SUMMATION_DTYPE
    )
    grad_key = jnp.einsum(
        "hqk,qhe->khe", grad_score, queries, preferred_element_type=SUMMATION_DTYPE
    )
    grad_value = jnp.einsum(
        "hqk,qhe->khe", prob_low, grad_ctx, preferred_element_type=SUMMATION_DTYPE
    )
    return (grad_query, grad_key, grad_value)


def body(
    hidden_in,
    cotangent,
    segment_ids,
    adapter_ids,
    ln_gain,
    ln_bias,
    w_qkv,
    b_qkv,
    w_out,
    b_out,
    w_fc1,
    b_fc1,
    w_fc2,
    b_fc2,
    down_input_factors,
    up_qkv,
    up_fc1,
    down_o,
    down_fc2,
    up_output_factors,
):
    hidden_full, cot_full = (
        lax.all_gather(hidden_in, "mp", axis=1, tiled=True),
        lax.all_gather(cotangent, "mp", axis=1, tiled=True),
    )
    (
        wide_qkv,
        wide_fc1,
        wide_out,
        wide_fc2,
        full_down_x,
        full_up_qkv,
        full_up_fc1,
        full_down_o,
        full_down_fc2,
        full_up_out,
    ) = (
        lax.all_gather(w_qkv, "dp", axis=0, tiled=True),
        lax.all_gather(w_fc1, "dp", axis=0, tiled=True),
        lax.all_gather(w_out, "dp", axis=1, tiled=True),
        lax.all_gather(w_fc2, "dp", axis=1, tiled=True),
        lax.all_gather(down_input_factors, "dp", axis=3, tiled=True),
        lax.all_gather(up_qkv, "dp", axis=1, tiled=True),
        lax.all_gather(up_fc1, "dp", axis=1, tiled=True),
        lax.all_gather(down_o, "dp", axis=1, tiled=True),
        lax.all_gather(down_fc2, "dp", axis=1, tiled=True),
        lax.all_gather(up_output_factors, "dp", axis=2, tiled=True),
    )
    seq_count = adapter_ids.shape[0]
    tok_count = hidden_in.shape[0]
    head_cols = b_qkv.shape[1]
    heads_local = head_cols // HEAD_DIM
    ff_local = b_fc1.shape[0]
    width_local = b_out.shape[0]
    column_start = lax.axis_index("mp") * width_local
    one_hot = (adapter_ids[:, None] == jnp.arange(NAD, dtype=jnp.int32)[None, :]).astype(
        jnp.bfloat16
    )

    def choose(table):
        picked = jnp.dot(one_hot, table.reshape(NAD, -1), preferred_element_type=SUMMATION_DTYPE)
        return picked.astype(jnp.bfloat16).reshape((seq_count,) + table.shape[1:])

    wide_in = hidden_full.astype(jnp.float32)
    mean_row = jnp.mean(wide_in, axis=-1, keepdims=True)
    centred = wide_in - mean_row
    inv_std = lax.rsqrt(jnp.mean(centred * centred, axis=-1, keepdims=True) + EPSILON)
    x_hat = centred * inv_std
    normed = (x_hat * ln_gain + ln_bias).astype(jnp.bfloat16)
    normalized_sequence = normed.reshape(seq_count, LEN, MODEL_WIDTH)
    selected_down_input = choose(full_down_x)
    sel_up_qkv = choose(full_up_qkv)
    sel_up_fc1 = choose(full_up_fc1)
    sel_down_o = choose(full_down_o)
    sel_down_fc2 = choose(full_down_fc2)
    selected_up_output = choose(full_up_out)
    lowrank_product = jnp.einsum(
        "mno,mgho->mngh",
        normalized_sequence,
        selected_down_input,
        preferred_element_type=SUMMATION_DTYPE,
    ).astype(jnp.bfloat16)
    qkv_pre = jnp.dot(
        normed, wide_qkv.reshape(MODEL_WIDTH, 3 * head_cols), preferred_element_type=SUMMATION_DTYPE
    ).reshape(seq_count, LEN, 3, head_cols)
    qkv_pre = (
        qkv_pre
        + b_qkv.astype(jnp.float32)
        + jnp.einsum(
            "sljr,srjh->sljh",
            lowrank_product[:, :, :3],
            sel_up_qkv,
            preferred_element_type=SUMMATION_DTYPE,
        )
    )
    cosine, sine = angles(segment_ids)
    head_shape = (seq_count, LEN, heads_local, HEAD_DIM)
    queries = (
        rotate(qkv_pre[:, :, 0].reshape(head_shape), cosine, sine, False) * HEAD_DIM ** (-0.5)
    ).astype(jnp.bfloat16)
    keys_low = rotate(qkv_pre[:, :, 1].reshape(head_shape), cosine, sine, False).astype(
        jnp.bfloat16
    )
    values_low = qkv_pre[:, :, 2].reshape(head_shape).astype(jnp.bfloat16)
    context, log_total = lax.map(attend, (queries, keys_low, values_low, segment_ids))
    context = context.reshape(tok_count, head_cols)
    fc1_extra = jnp.einsum(
        "slr,srf->slf", lowrank_product[:, :, 3], sel_up_fc1, preferred_element_type=SUMMATION_DTYPE
    ).reshape(tok_count, ff_local)
    fc1_pre = (
        jnp.dot(normed, wide_fc1, preferred_element_type=SUMMATION_DTYPE)
        + b_fc1.astype(jnp.float32)
        + fc1_extra
    )
    activated = gelu_tanh(fc1_pre).astype(jnp.bfloat16)
    context_seq = context.reshape(seq_count, LEN, head_cols)
    active_seq = activated.reshape(seq_count, LEN, ff_local)
    cotangent_sequence = cotangent.reshape(seq_count, LEN, width_local)
    branch_part = jnp.stack(
        [
            jnp.einsum(
                "slh,srh->slr", context_seq, sel_down_o, preferred_element_type=SUMMATION_DTYPE
            ),
            jnp.einsum(
                "slf,srf->slr", active_seq, sel_down_fc2, preferred_element_type=SUMMATION_DTYPE
            ),
        ],
        axis=2,
    )
    backward_portion = jnp.einsum(
        "hut,hnot->huno",
        cotangent_sequence,
        selected_up_output,
        preferred_element_type=SUMMATION_DTYPE,
    )
    branch_sum, back_sum = lax.psum((branch_part, backward_portion), "mp")
    branch_lowrank = branch_sum.astype(jnp.bfloat16)
    back_low = back_sum.astype(jnp.bfloat16)
    partial_rows = jnp.dot(context, wide_out, preferred_element_type=SUMMATION_DTYPE) + jnp.dot(
        activated, wide_fc2, preferred_element_type=SUMMATION_DTYPE
    )
    mixed = lax.psum_scatter(partial_rows, "mp", scatter_dimension=1, tiled=True)
    adapter_output = jnp.einsum(
        "fupz,fpzk->fuk", branch_lowrank, selected_up_output, preferred_element_type=SUMMATION_DTYPE
    ).reshape(tok_count, width_local)
    output = (
        hidden_in.astype(jnp.float32)
        + mixed
        + b_out.astype(jnp.float32)
        + b_fc2.astype(jnp.float32)
        + adapter_output
    ).astype(jnp.bfloat16)
    grad_context = (
        jnp.dot(cot_full, wide_out.T, preferred_element_type=SUMMATION_DTYPE)
        + jnp.einsum(
            "slr,srh->slh", back_low[:, :, 0], sel_down_o, preferred_element_type=SUMMATION_DTYPE
        ).reshape(tok_count, head_cols)
    ).astype(jnp.bfloat16)
    grad_active = jnp.dot(
        cot_full, wide_fc2.T, preferred_element_type=SUMMATION_DTYPE
    ) + jnp.einsum(
        "slr,srf->slf", back_low[:, :, 1], sel_down_fc2, preferred_element_type=SUMMATION_DTYPE
    ).reshape(
        tok_count, ff_local
    )
    gelu_value, gelu_back = jax.vjp(gelu_tanh, fc1_pre)
    grad_fc1 = gelu_back(grad_active)[0].astype(jnp.bfloat16)
    grad_query, grad_key, grad_value = lax.map(
        attend_back,
        (queries, keys_low, values_low, segment_ids, log_total, grad_context.reshape(head_shape)),
    )
    grad_query = rotate(grad_query * HEAD_DIM ** (-0.5), cosine, sine, True)
    grad_key = rotate(grad_key, cosine, sine, True)
    grad_qkv = (
        jnp.stack([grad_query, grad_key, grad_value], axis=2)
        .reshape(seq_count, LEN, 3, head_cols)
        .astype(jnp.bfloat16)
    )
    grad_fc1_seq = grad_fc1.reshape(seq_count, LEN, ff_local)
    rank_part = jnp.concatenate(
        [
            jnp.einsum(
                "sljh,srjh->sljr", grad_qkv, sel_up_qkv, preferred_element_type=SUMMATION_DTYPE
            ),
            jnp.einsum(
                "slf,srf->slr", grad_fc1_seq, sel_up_fc1, preferred_element_type=SUMMATION_DTYPE
            )[:, :, None],
        ],
        axis=2,
    )
    normed_part = jnp.dot(
        grad_qkv.reshape(tok_count, 3 * head_cols),
        wide_qkv.reshape(MODEL_WIDTH, 3 * head_cols).T,
        preferred_element_type=SUMMATION_DTYPE,
    ) + jnp.dot(grad_fc1, wide_fc1.T, preferred_element_type=SUMMATION_DTYPE)
    normed_sum, rank_sum = lax.psum((normed_part, rank_part), "mp")
    rank_reduced = rank_sum.astype(jnp.bfloat16)
    grad_normed = normed_sum + jnp.einsum(
        "cuxk,cxki->cui", rank_reduced, selected_down_input, preferred_element_type=SUMMATION_DTYPE
    ).reshape(tok_count, MODEL_WIDTH)
    scaled = grad_normed * ln_gain
    first_mean = jnp.mean(scaled, axis=-1, keepdims=True)
    second_mean = jnp.mean(scaled * x_hat, axis=-1, keepdims=True)
    grad_rows = inv_std * (scaled - first_mean - x_hat * second_mean)
    grad_local = lax.dynamic_slice_in_dim(grad_rows, column_start, width_local, axis=1)
    grad_in = (cotangent.astype(jnp.float32) + grad_local).astype(jnp.bfloat16)
    hot_wide = one_hot.astype(jnp.float32)

    def spread(picked):
        summed = jnp.dot(hot_wide.T, picked.reshape(seq_count, -1), precision=lax.Precision.HIGHEST)
        return summed.reshape((NAD,) + picked.shape[1:])

    grad_sel_down_x = jnp.einsum(
        "mexh,meb->mxhb", rank_reduced, normalized_sequence, preferred_element_type=SUMMATION_DTYPE
    )
    grad_sel_up_qkv = jnp.einsum(
        "sljr,sljh->srjh",
        lowrank_product[:, :, :3],
        grad_qkv,
        preferred_element_type=SUMMATION_DTYPE,
    )
    grad_sel_up_fc1 = jnp.einsum(
        "slr,slf->srf",
        lowrank_product[:, :, 3],
        grad_fc1_seq,
        preferred_element_type=SUMMATION_DTYPE,
    )
    grad_sel_down_o = jnp.einsum(
        "slr,slh->srh", back_low[:, :, 0], context_seq, preferred_element_type=SUMMATION_DTYPE
    )
    grad_sel_down_fc2 = jnp.einsum(
        "slr,slf->srf", back_low[:, :, 1], active_seq, preferred_element_type=SUMMATION_DTYPE
    )
    grad_sel_up_out = jnp.einsum(
        "mkbx,mko->mbxo", branch_lowrank, cotangent_sequence, preferred_element_type=SUMMATION_DTYPE
    )
    grad_down_x, grad_up_qkv, grad_up_fc1, grad_down_o, grad_down_fc2, grad_up_out = (
        lax.psum_scatter(spread(grad_sel_down_x), "dp", scatter_dimension=3, tiled=True),
        lax.psum_scatter(spread(grad_sel_up_qkv), "dp", scatter_dimension=1, tiled=True),
        lax.psum_scatter(spread(grad_sel_up_fc1), "dp", scatter_dimension=1, tiled=True),
        lax.psum_scatter(spread(grad_sel_down_o), "dp", scatter_dimension=1, tiled=True),
        lax.psum_scatter(spread(grad_sel_down_fc2), "dp", scatter_dimension=1, tiled=True),
        lax.psum_scatter(spread(grad_sel_up_out), "dp", scatter_dimension=2, tiled=True),
    )
    return (
        output,
        grad_in,
        grad_down_x,
        grad_up_qkv,
        grad_up_fc1,
        grad_down_o,
        grad_down_fc2,
        grad_up_out,
    )


def solution(mesh):
    in_specs = (
        P("dp", "mp"),
        P("dp", "mp"),
        P("dp", None),
        P("dp"),
        P(),
        P(),
        P("dp", None, "mp"),
        P(None, "mp"),
        P("mp", "dp"),
        P("mp"),
        P("dp", "mp"),
        P("mp"),
        P("mp", "dp"),
        P("mp"),
        P(None, None, None, "dp"),
        P(None, "dp", None, "mp"),
        P(None, "dp", "mp"),
        P(None, "dp", "mp"),
        P(None, "dp", "mp"),
        P(None, None, "dp", "mp"),
    )
    out_specs = (
        P("dp", "mp"),
        P("dp", "mp"),
        P(None, None, None, "dp"),
        P(None, "dp", None, "mp"),
        P(None, "dp", "mp"),
        P(None, "dp", "mp"),
        P(None, "dp", "mp"),
        P(None, None, "dp", "mp"),
    )
    return jax.shard_map(body, mesh=mesh, in_specs=in_specs, out_specs=out_specs, check_vma=False)
```

profile of v0, /device:TPU:0, one launch (start us, length us, event | category | flops | bytes accessed | tf_op | source)
XLA Modules:
  0.0 1502.1 jit_solution(14168439272285699542)
XLA Ops:
  13.7 33.7 %all_gather.38 = bf16[8,16,3,512]{3,0,2,1:T(8,128)(2,1)S(1)} all-gather(bf16[8,2,3,512]{3,0,2,1:T(8,128)(2,1)S(1)} %copy.138), channel_id=1, replica_groups=mesh['dp'=8,'mp'=4] {'dp'}, dimensions={1}, use_global_device_ids=true | all-gather | bytes 442368 | tf_op jit(solution)/shard_map/all_gather | solution.py:136
  49.2 31.4 %all_gather.46 = bf16[8,2,16,512]{3,0,1,2:T(8,128)(2,1)S(1)} all-gather(bf16[8,2,2,512]{3,0,1,2:T(8,128)(2,1)S(1)} %copy.145), channel_id=1, replica_groups=mesh['dp'=8,'mp'=4] {'dp'}, dimensions={2}, use_global_device_ids=true | all-gather | bytes 294912 | tf_op jit(solution)/shard_map/all_gather | solution.py:140
  82.5 19.8 %all-reduce.11 = bf16[2,1024,2,16]{1,3,2,0:T(8,128)(2,1)S(1)} all-reduce(f32[2,1024,2,16]{1,3,2,0:T(8,128)S(1)} %convolution_bitcast_fusion.3), channel_id=1, replica_groups=mesh['dp'=8,'mp'=4] {'mp'}, use_global_device_ids=true, to_apply=%region_10.11 | all-reduce | flops 65536 | bytes 393216 | tf_op jit(solution)/shard_map/psum | solution.py:229
  102.3 30.6 %all_gather.44 = bf16[8,16,512]{2,0,1:T(8,128)(2,1)S(1)} all-gather(bf16[8,2,512]{2,0,1:T(8,128)(2,1)S(1)} %copy.142), channel_id=1, replica_groups=mesh['dp'=8,'mp'=4] {'dp'}, dimensions={1}, use_global_device_ids=true | all-gather | bytes 147456 | tf_op jit(solution)/shard_map/all_gather | solution.py:138
  133.2 32.9 %all_gather.42 = bf16[8,16,2048]{2,0,1:T(8,128)(2,1)S(1)} all-gather(bf16[8,2,2048]{2,0,1:T(8,128)(2,1)S(1)} %copy.141), channel_id=1, replica_groups=mesh['dp'=8,'mp'=4] {'dp'}, dimensions={1}, use_global_device_ids=true | all-gather | bytes 589824 | tf_op jit(solution)/shard_map/all_gather | solution.py:137
  167.7 34.8 %all_gather.45 = bf16[8,16,2048]{2,0,1:T(8,128)(2,1)S(1)} all-gather(bf16[8,2,2048]{2,0,1:T(8,128)(2,1)S(1)} %copy.144), channel_id=1, replica_groups=mesh['dp'=8,'mp'=4] {'dp'}, dimensions={1}, use_global_device_ids=true | all-gather | bytes 589824 | tf_op jit(solution)/shard_map/all_gather | solution.py:139
  243.6 22.5 %bitcast_add_fusion.3 = f32[2,1024,3,512]{1,3,2,0:T(8,128)} fusion(f32[2,3,512,1024]{3,2,1,0:T(8,128)} %fusion.67, f32[3,512]{1,0:T(4,128)S(1)} %convert_element_type.115, bf16[2,1024,2048,1]{2,1,3,0:T(8,128)(2,1)} %bitcast.351, bf16[2048,3,512]{0,2,1:T(8,128)(2,1)} %all-gather.10.cloned.1.call-done), kind=kOutput, calls=%fused_computation.84 | convolution fusion | flops 12891193344 | bytes 39852032 | tf_op jit(solution)/shard_map/dot_general | solution.py:176
  277.6 91.2 %while.26 = (s32[]{:T(128)}, bf16[2,1024,8,64]{1,3,2,0:T(8,128)(2,1)}, f32[2,8,1024]{2,1,0:T(8,128)S(1)}, bf16[2,1024,8,64]{1,3,2,0:T(8,128)(2,1)}, s32[2,1024]{...) while((s32[]{:T(128)}, ...), condition=%wide.region_7.8_spmd, body=%wide.region_4.7_spmd.sunk | while | flops 2226642944 | bytes 117717112 | solution.py:198
  391.7 213.7 %while.27 = (s32[]{:T(128)}, f32[2,1024,8,64]{1,3,2,0:T(8,128)}, f32[2,1024,8,64]{1,3,2,0:T(8,128)}, bf16[2,1024,8,64]{1,3,2,0:T(8,128)(2,1)}, bf16[2,1024,8,64]...) while((s32[]{:T(128)}, f32[2,1024,8,64]{1,3,2,0:T(8,128)}, ...), condition=%wide.region_13.14_spmd, body=%wide.region_11.13_spmd.sunk | while | flops 5472509952 | bytes 286508192 | solution.py:261
  408.0 23.0 %multiply_reduce_fusion.3 = (f32[8,1024]{1,0:T(8,128)S(1)}, f32[8,1024,1024]{1,2,0:T(8,128)}) fusion(f32[8,1024,1024]{1,2,0:T(8,128)} %fusion.203, f32[8,1024]{1,0:T(8,128)S(1)} %dynamic-slice_bitcast_fusion.2, pred[1024,1024]{0,1:T(8,128)(4,1)S(1)} %fusion.204, bf16[2,1024,8,64]{1,3,2,0:T(8,128)(2,1)S(1)} %copy-done.9, s32[]{:T(128)} %get-tuple-element.406, ...), kind=kOutput, calls=%fused_computation.23.clone.1 | convolution fusion | flops 1107288064 | bytes 70321152 | tf_op jit(solution)/shard_map/while/body/eval_jaxpr/qhe,khe->hqk/dot_general | solution.py:76
  431.0 28.6 %multiply_convert_fusion.3 = bf16[8,1024,1024]{1,2,0:T(8,128)(2,1)} fusion(f32[8,1024,1024]{1,2,0:T(8,128)} %get-tuple-element.369, f32[8,1024,1024]{1,2,0:T(8,128)} %fusion.203, f32[8,1024]{1,0:T(8,128)S(1)} %get-tuple-element.370, f32[8,1024]{1,0:T(8,128)S(1)} %dynamic-slice_bitcast_fusion.2, pred[1024,1024]{0,1:T(8,128)(4,1)S(1)} %fusion.204), kind=kLoop, calls=%fused_computation.22.clone.1 | loop fusion | flops 41943040 | bytes 85000192 | tf_op jit(solution)/shard_map/while/body/eval_jaxpr/convert_element_type | solution.py:80
  514.3 23.2 %multiply_reduce_fusion.3 = (f32[8,1024]{1,0:T(8,128)S(1)}, f32[8,1024,1024]{1,2,0:T(8,128)}) fusion(f32[8,1024,1024]{1,2,0:T(8,128)} %fusion.203, f32[8,1024]{1,0:T(8,128)S(1)} %dynamic-slice_bitcast_fusion.2, pred[1024,1024]{0,1:T(8,128)(4,1)S(1)} %fusion.204, bf16[2,1024,8,64]{1,3,2,0:T(8,128)(2,1)S(1)} %copy-done.9, s32[]{:T(128)} %get-tuple-element.406, ...), kind=kOutput, calls=%fused_computation.23.clone.1 | convolution fusion | flops 1107288064 | bytes 70321152 | tf_op jit(solution)/shard_map/while/body/eval_jaxpr/qhe,khe->hqk/dot_general | solution.py:76
  537.6 28.8 %multiply_convert_fusion.3 = bf16[8,1024,1024]{1,2,0:T(8,128)(2,1)} fusion(f32[8,1024,1024]{1,2,0:T(8,128)} %get-tuple-element.369, f32[8,1024,1024]{1,2,0:T(8,128)} %fusion.203, f32[8,1024]{1,0:T(8,128)S(1)} %get-tuple-element.370, f32[8,1024]{1,0:T(8,128)S(1)} %dynamic-slice_bitcast_fusion.2, pred[1024,1024]{0,1:T(8,128)(4,1)S(1)} %fusion.204), kind=kLoop, calls=%fused_computation.22.clone.1 | loop fusion | flops 41943040 | bytes 85000192 | tf_op jit(solution)/shard_map/while/body/eval_jaxpr/convert_element_type | solution.py:80
  647.6 31.3 %multiply_convert_fusion.1 = (bf16[2048,2048]{1,0:T(8,128)(2,1)}, f32[2048,2048]{1,0:T(8,128)}) fusion(f32[2,1024,2048]{2,1,0:T(8,128)} %fusion.73, f32[2048]{0:T(1024)S(1)} %copy-done.51, bf16[2048,2048]{1,0:T(8,128)(2,1)} %copy-done.4, bf16[2048,2048]{1,0:T(8,128)(2,1)} %all-gather.16.cloned.1.call-done), kind=kOutput, calls=%fused_computation.82 | convolution fusion | flops 17226006528 | bytes 58728448 | tf_op jit(solution)/shard_map/dot_general | solution.py:204
  678.9 39.3 %fusion.51 = bf16[2048,2048]{1,0:T(8,128)(2,1)S(1)} fusion(f32[2048,2048]{1,0:T(8,128)} %get-tuple-element.256, f32[2,1024,2048]{2,1,0:T(8,128)} %fusion.69, bf16[2048,2048]{1,0:T(8,128)(2,1)} %all-gather.20.cloned.1.call-done, bf16[2048,2048]{1,0:T(8,128)(2,1)} %all-gather.18.cloned.1.call-done), kind=kOutput, calls=%fused_computation.74 | convolution fusion | flops 17284726784 | bytes 58720256 | tf_op jit(solution)/shard_map/dot_general | solution.py:252
  726.9 19.7 %all-reduce.12 = (bf16[2,1024,2,16]{1,3,0,2:T(8,128)(2,1)}, bf16[2,1024,4,16]{1,3,2,0:T(8,128)(2,1)S(1)}) all-reduce(f32[2,1024,2,16]{1,3,0,2:T(8,128)S(1)} %pad_maximum_fusion.5, f32[2,1024,4,16]{1,3,2,0:T(8,128)S(1)} %pad_maximum_fusion.4), channel_id=1, replica_groups=mesh['dp'=8,'mp'=4] {'mp'}, use_global_device_ids=true, to_apply=%region_9.10 | all-reduce | flops 196608 | bytes 1179648 | tf_op jit(solution)/shard_map/psum | solution.py:229
  811.4 26.4 %convolution_add_fusion = f32[2048,2048]{1,0:T(8,128)} fusion(f32[2048,2048]{1,0:T(8,128)} %fusion.130, bf16[2048,2048]{1,0:T(8,128)(2,1)} %copy-done.3, bf16[2048,2048]{1,0:T(8,128)(2,1)} %all-gather.16.cloned.1.call-done), kind=kOutput, calls=%fused_computation.86 | convolution fusion | flops 17184063488 | bytes 50331648 | tf_op jit(solution)/shard_map/dot_general | solution.py:288
  850.6 23.7 %convolution_add_fusion.1 = f32[2048,2048]{1,0:T(8,128)} fusion(f32[2048,2048]{1,0:T(8,128)} %fusion.129, bf16[2048,2048]{1,0:T(8,128)(2,1)S(1)} %bitcast.347, bf16[2048,2048]{1,0:T(8,128)(2,1)} %all-gather.18.cloned.1.call-done), kind=kOutput, calls=%fused_computation.87 | convolution fusion | flops 17184063488 | bytes 50331648 | tf_op jit(solution)/shard_map/dot_general | solution.py:232
  891.8 21.4 %reduce-scatter.14.cloned.1.call-done = f32[8,2,2048]{2,0,1:T(8,128)} async-done(((f32[8,16,2048]{2,0,1:T(8,128)}), f32[8,2,2048]{2,0,1:T(8,128)}) %reduce-scatter.14.cloned.1.call-update) | async-done | bytes 131088 | tf_op jit(solution)/shard_map/reduce_scatter | solution.py:333
  914.8 64.8 %reduce-scatter.18.cloned.1.call-done = f32[8,2,2048]{2,0,1:T(8,128)} async-done(((f32[8,16,2048]{2,0,1:T(8,128)}), f32[8,2,2048]{2,0,1:T(8,128)}) %reduce-scatter.18.cloned.1.call-update) | async-done | bytes 131088 | tf_op jit(solution)/shard_map/reduce_scatter | solution.py:335
  981.3 89.7 %reduce-scatter.10.cloned.1.call-done = f32[8,4,16,256]{3,0,2,1:T(8,128)} async-done(((f32[8,4,16,2048]{3,0,2,1:T(8,128)}), f32[8,4,16,256]{3,0,2,1:T(8,128)}) %reduce-scatter.10.cloned.1.call-update) | async-done | bytes 524304 | tf_op jit(solution)/shard_map/reduce_scatter | solution.py:331
  1073.0 288.3 %all-reduce.8.cloned.1.call-done = f32[2048,2048]{1,0:T(8,128)} async-done(((f32[2048,2048]{1,0:T(8,128)}), f32[2048,2048]{1,0:T(8,128)}) %all-reduce.8.cloned.1.call-update) | async-done | bytes 16777232 | tf_op jit(solution)/shard_map/psum | solution.py:289
  1361.3 30.5 %fusion.120 = (f32[2048]{0:T(1024)S(1)}, f32[2048]{0:T(1024)S(1)}, f32[2048,2048]{1,0:T(8,128)}, f32[2048,2048]{1,0:T(8,128)}) fusion(f32[2048]{0:T(1024)S(1)} %copy-done.38, f32[2048]{0:T(1024)S(1)} %copy-done.40, bf16[2048,2048]{1,0:T(8,128)(2,1)} %all-gather.8.cloned.1.call-done, f32[2048]{0:T(1024)S(1)} %copy-done.47, ...), kind=kLoop, calls=%fused_computation.203 | loop fusion | flops 33550336 | bytes 75538432 | tf_op jit(solution)/shard_map/reduce_sum | solution.py:295
  1396.9 91.8 %reduce-scatter.8.cloned.1.call-done = f32[2048,512]{1,0:T(8,128)} async-done(((f32[2048,2048]{1,0:T(8,128)}), f32[2048,512]{1,0:T(8,128)}) %reduce-scatter.8.cloned.1.call-update) | async-done | bytes 4194320 | tf_op jit(solution)/shard_map/reduce_scatter | solution.py:235
  (307 shorter events, 449.4 us)
Async XLA Ops:
  7.2 125.9 %copy-start.43 = (bf16[8,2,2048]{2,1,0:T(2,128)(2,1)S(1)}, bf16[8,2,2048]{2,1,0:T(2,128)(2,1)}, u32[]{:S(2)}) copy-start(bf16[8,2,2048]{2,1,0:T(2,128)(2,1)} %param.40) | copy-start | bytes 196612
  7.3 207.2 %all-gather.12.cloned.1.call-start = ((), (), s32[]{:S(2)}) async-start(), calls=%async_computation.8 | async-start | bytes 2359296 | tf_op jit(solution)/shard_map/all_gather | solution.py:135
  8.0 159.1 %copy-start.53 = (bf16[2048]{0:T(1024)(128)(2,1)S(1)}, bf16[2048]{0:T(1024)(128)(2,1)}, u32[]{:S(2)}) copy-start(bf16[2048]{0:T(1024)(128)(2,1)} %param.35) | copy-start | bytes 12292
  8.0 159.7 %copy-start.44 = (bf16[8,2,2048]{2,1,0:T(2,128)(2,1)S(1)}, bf16[8,2,2048]{2,1,0:T(2,128)(2,1)}, u32[]{:S(2)}) copy-start(bf16[8,2,2048]{2,1,0:T(2,128)(2,1)} %param.42) | copy-start | bytes 196612
  8.0 210.3 %all-gather.8.cloned.1.call-start = ((), (), s32[]{:S(2)}) async-start(), calls=%async_computation.6 | async-start | bytes 10485760 | tf_op jit(solution)/shard_map/all_gather | solution.py:116
  8.8 234.9 %all-gather.10.cloned.1.call-start = ((), (), s32[]{:S(2)}) async-start(), calls=%async_computation.7 | async-start | bytes 7077888 | tf_op jit(solution)/shard_map/all_gather | solution.py:131
  11.1 357.7 %all-gather.14.cloned.1.call-start = ((), (), s32[]{:S(2)}) async-start(), calls=%async_computation.9 | async-start | bytes 2359296 | tf_op jit(solution)/shard_map/all_gather | solution.py:133
  11.7 357.1 %all-gather.20.cloned.1.call-start = ((), (), s32[]{:S(2)}) async-start(), calls=%async_computation.13 | async-start | bytes 10485760 | tf_op jit(solution)/shard_map/all_gather | solution.py:117
  12.3 635.3 %all-gather.16.cloned.1.call-start = ((), (), s32[]{:S(2)}) async-start(), calls=%async_computation.10 | async-start | bytes 9437184 | tf_op jit(solution)/shard_map/all_gather | solution.py:132
  12.9 666.0 %all-gather.18.cloned.1.call-start = ((), (), s32[]{:S(2)}) async-start(), calls=%async_computation.11 | async-start | bytes 9437184 | tf_op jit(solution)/shard_map/all_gather | solution.py:134
  13.6 862.6 %reduce-scatter.16.cloned.1.call-start = ((), (), s32[]{:S(2)}) async-start(), calls=%async_computation.18 | async-start | bytes 294912 | tf_op jit(solution)/shard_map/reduce_scatter | solution.py:334
  47.9 188.6 %copy-start.26 = (bf16[2,16,3,512]{3,2,1,0:T(4,128)(2,1)}, bf16[2,16,3,512]{3,2,1,0:T(4,128)(2,1)S(1)}, u32[]{:S(2)}) copy-start(bf16[2,16,3,512]{3,2,1,0:T(4,128)(2,1)S(1)} %reshape.324) | copy-start | bytes 294916
  102.3 111.6 %copy-start.13 = (bf16[2,1024,2,16]{1,3,2,0:T(8,128)(2,1)}, bf16[2,1024,2,16]{1,3,2,0:T(8,128)(2,1)S(1)}, u32[]{:S(2)}) copy-start(bf16[2,1024,2,16]{1,3,2,0:T(8,128)(2,1)S(1)} %all-reduce.11) | copy-start | bytes 393220
  641.1 236.5 %reduce-scatter.12.cloned.1.call-start = ((), (), s32[]{:S(2)}) async-start(), calls=%async_computation.16 | async-start | bytes 884736 | tf_op jit(solution)/shard_map/reduce_scatter | solution.py:332
  647.5 242.8 %all-reduce.10.cloned.1.call-start = ((), (), s32[]{:S(2)}) async-start(), calls=%async_computation.20 | async-start | bytes 1048576
  749.5 163.7 %reduce-scatter.14.cloned.1.call-start = ((), (), s32[]{:S(2)}) async-start(), calls=%async_computation.17 | async-start | bytes 1179648 | tf_op jit(solution)/shard_map/reduce_scatter | solution.py:333
  756.0 223.6 %reduce-scatter.18.cloned.1.call-start = ((), (), s32[]{:S(2)}) async-start(), calls=%async_computation.19 | async-start | bytes 1179648 | tf_op jit(solution)/shard_map/reduce_scatter | solution.py:335
  762.6 308.4 %reduce-scatter.10.cloned.1.call-start = ((), (), s32[]{:S(2)}) async-start(), calls=%async_computation.15 | async-start | bytes 4718592 | tf_op jit(solution)/shard_map/reduce_scatter | solution.py:331
  772.5 588.8 %all-reduce.8.cloned.1.call-start = ((), (), s32[]{:S(2)}) async-start(), calls=%async_computation.14 | async-start | bytes 33554432 | tf_op jit(solution)/shard_map/psum | solution.py:289
  837.9 650.8 %reduce-scatter.8.cloned.1.call-start = ((), (), s32[]{:S(2)}) async-start(), calls=%async_computation.12 | async-start | bytes 20971520 | tf_op jit(solution)/shard_map/reduce_scatter | solution.py:235
  882.1 479.2 %copy-start.38 = (f32[2048]{0:T(1024)S(1)}, f32[2048]{0:T(1024)}, u32[]{:S(2)}) copy-start(f32[2048]{0:T(1024)} %copy-done.37) | copy-start | bytes 24580
  882.1 479.2 %copy-start.40 = (f32[2048]{0:T(1024)S(1)}, f32[2048]{0:T(1024)}, u32[]{:S(2)}) copy-start(f32[2048]{0:T(1024)} %copy-done.39) | copy-start | bytes 24580
  882.1 479.2 %copy-start.47 = (f32[2048]{0:T(1024)S(1)}, f32[2048]{0:T(1024)}, u32[]{:S(2)}) copy-start(f32[2048]{0:T(1024)} %param.28) | copy-start | bytes 24580
  1073.0 318.8 %copy-start.7 = (bf16[2048,512]{1,0:T(8,128)(2,1)S(1)}, bf16[2048,512]{1,0:T(8,128)(2,1)}, u32[]{:S(2)}) copy-start(bf16[2048,512]{1,0:T(8,128)(2,1)} %param.25) | copy-start | bytes 6291460
  (56 other events, 919.7 us)
Sparse Core Ops, SparseCore 0:
  10.1 57.3 all-gather.11
  69.1 61.3 all-gather.7
  133.0 109.5 all-gather.9
  244.6 48.6 all-gather.13
  294.7 56.4 all-gather.19
  353.2 124.4 all-gather.15
  479.8 123.1 all-gather.17
  641.2 63.8 reduce-scatter.15
  708.4 62.1 reduce-scatter.11
  773.9 71.8 all-reduce.9
  849.7 63.3 reduce-scatter.13
  916.4 63.1 reduce-scatter.17
  983.3 87.6 reduce-scatter.9
  1073.4 287.9 all-reduce.7
  1363.8 124.8 reduce-scatter.7
where the time goes:
time: 1510 us; the launch traced here: 1500 us
  waiting for transfers between devices  560 us (37%)
  matrix products  477 us (32%)
  blocking collectives  203 us (13%)
  other arithmetic  156 us (10%)
  local copies, waits for them, and re-layouts  89.5 us (6%)
  between operations  15.7 us (1%)
    psum x1, waiting for transfers between devices, body(): normed_sum, rank_sum = lax.psum((normed_part, rank_part), 'mp')  288 us
    reduce_scatter x1, waiting for transfers between devices, body(): lax.psum_scatter(partial_rows, 'mp', scatter_dimension=1, tiled=True)  91.8 us
    reduce_scatter x1, waiting for transfers between devices, body(): lax.psum_scatter(spread(grad_sel_down_x), 'dp', scatter_dimension=3, tile...  89.7 us
    reduce_scatter x1, waiting for transfers between devices, body(): lax.psum_scatter(spread(grad_sel_down_fc2), 'dp', scatter_dimension=1, ti...  64.8 us
    dot_general x4, matrix products, masked_scores(): jnp.einsum('qhe,khe->hqk', queries, keys_low, preferred_element_type=SUMM...  59.4 us
    convert_element_type x2, other arithmetic, attend_back(): grad_score = (probs * (grad_prob - delta_row)).astype(jnp.bfloat16)  57.4 us
    dot_general x2, matrix products, attend_back(): jnp.einsum('qhe,khe->hqk', grad_ctx, values_low, preferred_element_type=S...  46.3 us
    psum x2, blocking collectives, body(): branch_sum, back_sum = lax.psum((branch_part, backward_portion), 'mp')  39.5 us
  transfers between devices with their start and end apart: 15, of which 5 were waited for; matrix products, arithmetic and copies ran while one was open for 47% of the time, Pallas kernels for 0%

commit v1 on v0

v1 whole, which is shorter than its diff:
```python
import jax
import jax.numpy as jnp
from jax import lax
from jax.experimental import pallas as pl
from jax.experimental.pallas import tpu as pltpu
from jax.sharding import PartitionSpec as P

MODEL_WIDTH = 2048
HEAD_DIM = 64
ROT = 32
NAD = 8
LEN = 1024
RANK = 16


EPSILON = 1e-05
GELU_C = 0.7978845608028654
SUMMATION_DTYPE = jnp.float32


def doc_starts(segments):
    places = jnp.arange(segments.shape[1], dtype=jnp.int32)
    change = jnp.concatenate(
        [jnp.ones((segments.shape[0], 1), dtype=bool), segments[:, 1:] != segments[:, :-1]], axis=1
    )
    return lax.cummax(jnp.where(change, places[None, :], 0), axis=1)


def turn_table(starts):
    places = jnp.arange(starts.shape[1], dtype=jnp.int32)
    offsets = (places[None, :] - starts).astype(jnp.float32).reshape(-1, 1)
    inverse_freq = 10000.0 ** (-2.0 * jnp.arange(ROT // 2, dtype=jnp.float32) / ROT)
    phase = offsets * inverse_freq
    cosine, sine = jnp.cos(phase), jnp.sin(phase)
    rest = jnp.ones((phase.shape[0], HEAD_DIM - ROT), jnp.float32)
    none, zero = jnp.zeros_like(rest), jnp.zeros_like(sine)
    heads = PAIR // HEAD_DIM
    return jnp.stack(
        [
            jnp.concatenate([cosine, cosine, rest] * heads, axis=1),
            jnp.concatenate([sine, zero, none] * heads, axis=1),
            jnp.concatenate([zero, sine, none] * heads, axis=1),
        ]
    )


PAIR = 2 * HEAD_DIM
BLOCK_Q = 256
REACH = 512


def spans():
    for start in range(0, LEN, BLOCK_Q):
        yield start, max(0, start - REACH), start + BLOCK_Q


def masked_exp_args(score, doc_ref, start, low, high):
    keys = lax.broadcasted_iota(jnp.int32, (high - low, BLOCK_Q), 0) + low
    asks = lax.broadcasted_iota(jnp.int32, (high - low, BLOCK_Q), 1) + start
    first = doc_ref[0, :, start : start + BLOCK_Q]
    return jnp.where((keys >= first) & (keys <= asks), score, -1e30)


def dot_tt(left, right):
    return lax.dot_general(
        left, right, (((1,), (1,)), ((), ())), preferred_element_type=SUMMATION_DTYPE
    )


def head_only(rows, head):
    lanes = lax.broadcasted_iota(jnp.int32, rows.shape, 1)
    return jnp.where(lanes // HEAD_DIM == head, rows, jnp.zeros_like(rows))


def attend_kernel(doc_ref, q_ref, k_ref, v_ref, out_ref, log_ref):
    values_t = v_ref[...].astype(jnp.float32).T.astype(jnp.bfloat16)
    for start, low, high in spans():
        parts = []
        for head in range(2):
            ask = head_only(q_ref[start : start + BLOCK_Q, :], head)
            score = masked_exp_args(dot_tt(k_ref[low:high, :], ask), doc_ref, start, low, high)
            top = jnp.max(score, axis=0, keepdims=True)
            raised = jnp.exp(score - top)
            total = jnp.sum(raised, axis=0, keepdims=True)
            mix = jnp.dot(
                values_t[head * HEAD_DIM : (head + 1) * HEAD_DIM, low:high],
                raised.astype(jnp.bfloat16),
                preferred_element_type=SUMMATION_DTYPE,
            )
            parts.append(mix / total)
            log_ref[0, 0, head : head + 1, start : start + BLOCK_Q] = top + jnp.log(total)
        out_ref[start : start + BLOCK_Q, :] = jnp.concatenate(parts, axis=0).T.astype(jnp.bfloat16)


def turn(rows, table_ref, inverse):
    half = ROT // 2
    wide = rows.shape[1]
    plus = pltpu.roll(rows, wide - half, axis=1)
    minus = pltpu.roll(rows, half, axis=1)
    cosine, first_sine, second_sine = table_ref[0], table_ref[1], table_ref[2]
    if inverse:
        return rows * cosine + plus * first_sine - minus * second_sine
    return rows * cosine - plus * first_sine + minus * second_sine


def attend_back_kernel(
    doc_ref, q_ref, k_ref, v_ref, g_ref, log_ref, table_ref, dq_ref, dk_ref, dv_ref,
    sum_q, sum_k, sum_v,
):
    keys_t = k_ref[...].astype(jnp.float32).T.astype(jnp.bfloat16)
    sum_k[...] = jnp.zeros_like(sum_k)
    sum_v[...] = jnp.zeros_like(sum_v)
    for start, low, high in spans():
        here = slice(start, start + BLOCK_Q)
        for head in range(2):
            ask = head_only(q_ref[here, :], head)
            grad = head_only(g_ref[here, :], head)
            score = masked_exp_args(dot_tt(k_ref[low:high, :], ask), doc_ref, start, low, high)
            probs = jnp.exp(score - log_ref[0, 0, head : head + 1, here])
            grad_probs = dot_tt(v_ref[low:high, :], grad)
            delta = jnp.sum(probs * grad_probs, axis=0, keepdims=True)
            grad_score = (probs * (grad_probs - delta)).astype(jnp.bfloat16)
            sum_v[low:high, :] += jnp.dot(
                probs.astype(jnp.bfloat16), grad, preferred_element_type=SUMMATION_DTYPE
            )
            sum_k[low:high, :] += jnp.dot(
                grad_score, ask, preferred_element_type=SUMMATION_DTYPE
            )
            sum_q[head * HEAD_DIM : (head + 1) * HEAD_DIM, here] = jnp.dot(
                keys_t[head * HEAD_DIM : (head + 1) * HEAD_DIM, low:high],
                grad_score,
                preferred_element_type=SUMMATION_DTYPE,
            )
    scale = HEAD_DIM ** (-0.5)
    dq_ref[...] = turn(sum_q[...].T * scale, table_ref, True).astype(jnp.bfloat16)
    dk_ref[...] = turn(sum_k[...], table_ref, True).astype(jnp.bfloat16)
    dv_ref[...] = sum_v[...].astype(jnp.bfloat16)


def attention_specs(seq_count, pairs):
    rows = pl.BlockSpec((LEN, PAIR), lambda s, p: (s, p))
    doc = pl.BlockSpec((1, 1, LEN), lambda s, p: (s, 0, 0))
    logs = pl.BlockSpec((1, 1, 2, LEN), lambda s, p: (s, p, 0, 0))
    table = pl.BlockSpec((3, LEN, PAIR), lambda s, p: (0, s, 0))
    return rows, doc, logs, table


def attention(doc, queries, keys, values):
    seq_count = doc.shape[0]
    pairs = queries.shape[1] // PAIR
    rows, docs, logs, _ = attention_specs(seq_count, pairs)
    area = seq_count * pairs * 2 * 9 * BLOCK_Q * BLOCK_Q
    return pl.pallas_call(
        attend_kernel,
        grid=(seq_count, pairs),
        in_specs=[docs, rows, rows, rows],
        out_specs=[rows, logs],
        out_shape=[
            jax.ShapeDtypeStruct(queries.shape, jnp.bfloat16),
            jax.ShapeDtypeStruct((seq_count, pairs, 2, LEN), jnp.float32),
        ],
        cost_estimate=pl.CostEstimate(
            flops=area * 4 * PAIR, bytes_accessed=queries.size * 8, transcendentals=area
        ),
        name="attend",
    )(doc, queries, keys, values)


def attention_back(doc, queries, keys, values, grad, logs_in, table):
    seq_count = doc.shape[0]
    pairs = queries.shape[1] // PAIR
    rows, docs, logs, tables = attention_specs(seq_count, pairs)
    area = seq_count * pairs * 2 * 9 * BLOCK_Q * BLOCK_Q
    return pl.pallas_call(
        attend_back_kernel,
        grid=(seq_count, pairs),
        in_specs=[docs, rows, rows, rows, rows, logs, tables],
        out_specs=[rows, rows, rows],
        out_shape=[jax.ShapeDtypeStruct(queries.shape, jnp.bfloat16)] * 3,
        scratch_shapes=[
            pltpu.VMEM((PAIR, LEN), jnp.float32),
            pltpu.VMEM((LEN, PAIR), jnp.float32),
            pltpu.VMEM((LEN, PAIR), jnp.float32),
        ],
        cost_estimate=pl.CostEstimate(
            flops=area * 10 * PAIR, bytes_accessed=queries.size * 14, transcendentals=area
        ),
        name="attend_back",
    )(doc, queries, keys, values, grad, logs_in, table)


def ring_order(count):
    inner = 2 if count <= 8 else 4
    outer = max(count // inner, 1)
    if count % inner:
        return list(range(count))
    order = [z * inner for z in range(outer)]
    for z in range(outer - 1, -1, -1):
        rest = list(range(1, inner))
        if (outer - 1 - z) % 2:
            rest = rest[::-1]
        order += [z * inner + y for y in rest]
    return order


def ring_gather(block, count, axis, rows):
    order = ring_order(count)
    place = [order.index(i) for i in range(count)]
    ahead = [(order[i], order[(i + 1) % count]) for i in range(count)]
    back = [(b, a) for a, b in ahead]
    me = jnp.asarray(place, jnp.int32)[lax.axis_index("dp")]
    table = jnp.asarray(order, jnp.int32)
    half = block.shape[rows] // 2
    size = block.shape[axis]
    shape = list(block.shape)
    shape[axis] = size * count
    out = jnp.zeros(shape, block.dtype)
    down, up = count // 2, count - 1 - count // 2
    found = []
    for part in range(2):
        piece = lax.slice_in_dim(block, part * half, (part + 1) * half, axis=rows)
        found.append((part, 0, piece))
        for route, sign, hops in ((ahead, -1, (down, up)[part]), (back, 1, (up, down)[part])):
            moving = piece
            for hop in range(1, hops + 1):
                moving = lax.ppermute(moving, "dp", route)
                found.append((part, sign * hop, moving))
    for part, shift, piece in sorted(found, key=lambda f: abs(f[1])):
        source = table[lax.rem(me + shift + count, count)]
        start = [0] * block.ndim
        start[rows] = part * half
        start[axis] = start[axis] + source * size
        out = lax.dynamic_update_slice(out, piece, start)
    return out


def swap(value, axis, count, bit):
    return lax.ppermute(value, axis, [(i, i ^ bit) for i in range(count)])


def bits_of(count):
    return [1 << b for b in range(count.bit_length() - 1)]


def pieces_of(block, count):
    pieces = {0: block}
    for bit in reversed(bits_of(count)):
        for key in list(pieces):
            pieces[key ^ bit] = swap(pieces[key], "mp", count, bit)
    return [pieces[k] for k in range(count)]


def lay_out(pieces, axis):
    me = lax.axis_index("mp")
    size = pieces[0].shape[axis]
    out = jnp.concatenate(pieces, axis=axis)
    for key, piece in enumerate(pieces):
        out = lax.dynamic_update_slice_in_dim(out, piece, (me ^ key) * size, axis=axis)
    return out


def sum_over_mp(value, count):
    for bit in bits_of(count):
        value = value + swap(value, "mp", count, bit)
    return value


def share_out(partial, count):
    me = lax.axis_index("mp")
    width = partial.shape[1] // count
    kept = partial
    for bit in bits_of(count):
        ahead = kept.shape[1] // (2 * width)
        mine = lax.rem(me // bit, 2)
        grid = kept.reshape(kept.shape[0], ahead, 2, width)
        give = lax.dynamic_index_in_dim(grid, 1 - mine, 2, keepdims=False)
        keep = lax.dynamic_index_in_dim(grid, mine, 2, keepdims=False)
        got = swap(give.reshape(-1, ahead * width).astype(jnp.bfloat16), "mp", count, bit)
        kept = keep.reshape(-1, ahead * width) + got.astype(jnp.float32)
    return kept


def shift_dp(value, count, shift):
    return lax.ppermute(value, "dp", [(i, (i + shift) % count) for i in range(count)])


def in_order(received, count):
    rolled = jnp.stack(received[::-1] * 2)
    start = count - 1 - lax.axis_index("dp")
    return lax.dynamic_slice_in_dim(rolled, start, count, axis=0)


def one_hot(ids):
    return (ids[:, None] == jnp.arange(NAD, dtype=jnp.int32)[None, :]).astype(jnp.bfloat16)


def dot(left, right):
    return jnp.dot(left, right, preferred_element_type=SUMMATION_DTYPE)


def sums(spec, left, right):
    return jnp.einsum(spec, left, right, preferred_element_type=SUMMATION_DTYPE)


def gelu_tanh(values):
    return 0.5 * values * (1.0 + jnp.tanh(GELU_C * (values + 0.044715 * values * values * values)))


def gelu_slope(values):
    square = values * values
    bend = jnp.tanh(GELU_C * (values + 0.044715 * values * square))
    return 0.5 * (1.0 + bend) + 0.5 * values * (1.0 - bend * bend) * (
        GELU_C * (1.0 + 3.0 * 0.044715 * square)
    )


def turned(rows, table, heads):
    half = ROT // 2
    cosine, first_sine, second_sine = [
        jnp.concatenate([t] * (heads * HEAD_DIM // PAIR), axis=1) for t in table
    ]
    plus = jnp.roll(rows, -half, axis=1)
    minus = jnp.roll(rows, half, axis=1)
    return rows * cosine - plus * first_sine + minus * second_sine


def make_body(n_dp, n_mp):
    def body(
        hidden_in, cotangent, segment_ids, adapter_ids, ln_gain, ln_bias, w_qkv, b_qkv, w_out,
        b_out, w_fc1, b_fc1, w_fc2, b_fc2, down_input_factors, up_qkv, up_fc1, down_o, down_fc2,
        up_output_factors,
    ):
        seqs = adapter_ids.shape[0]
        tokens = hidden_in.shape[0]
        head_cols = b_qkv.shape[1]
        ff_cols = b_fc1.shape[0]
        width = b_out.shape[0]
        ranks = up_fc1.shape[1]
        features = down_input_factors.shape[3]
        me = lax.axis_index("mp")

        ids = [adapter_ids] + [shift_dp(adapter_ids, n_dp, k) for k in range(1, n_dp)]
        tables = [down_input_factors, up_qkv, up_fc1, down_o, down_fc2, up_output_factors]
        packed = jnp.concatenate([t.reshape(NAD, -1) for t in tables], axis=1)
        asked = jnp.concatenate([ids[(n_dp - k) % n_dp] for k in range(n_dp)])
        picked = dot(one_hot(asked), packed).astype(jnp.bfloat16).reshape(n_dp, seqs, -1)
        got = [picked[0]] + [shift_dp(picked[k], n_dp, k) for k in range(1, n_dp)]
        mine = in_order(got, n_dp)
        cut, spot = [], 0
        for t in tables:
            size = t.size // NAD
            cut.append(mine[:, :, spot : spot + size].reshape((n_dp, seqs) + t.shape[1:]))
            spot += size
        rank = n_dp * ranks
        a_in = jnp.moveaxis(cut[0], 0, 3).reshape(seqs, 4 * rank, MODEL_WIDTH)
        u_qkv = jnp.moveaxis(cut[1], 0, 1).reshape(seqs, rank, 3, head_cols)
        u_fc1 = jnp.moveaxis(cut[2], 0, 1).reshape(seqs, rank, ff_cols)
        a_o = jnp.moveaxis(cut[3], 0, 1).reshape(seqs, rank, head_cols)
        a_fc2 = jnp.moveaxis(cut[4], 0, 1).reshape(seqs, rank, ff_cols)
        u_out = jnp.moveaxis(cut[5], 0, 2).reshape(seqs, 2 * rank, width)
        u_block = jnp.concatenate(
            [
                jnp.pad(u_qkv[:, :, j], ((0, 0), (0, 0), (j * head_cols, (2 - j) * head_cols)))
                for j in range(3)
            ],
            axis=1,
        )

        hidden_full = lay_out(pieces_of(hidden_in, n_mp), 1)
        wide_qkv = ring_gather(w_qkv.reshape(features, 3 * head_cols), n_dp, 0, 0)
        cot_full = lay_out(pieces_of(cotangent, n_mp), 1)
        wide_out = ring_gather(w_out, n_dp, 1, 0)
        wide_fc1 = lax.all_gather(w_fc1, "dp", axis=0, tiled=True)
        wide_fc2 = lax.all_gather(w_fc2, "dp", axis=1, tiled=True)

        def by_seq(rows):
            return rows.reshape(seqs, LEN, rows.shape[1])

        starts = doc_starts(segment_ids)
        table = turn_table(starts)
        doc = starts[:, None, :]
        cot_seq = by_seq(cotangent)
        back_sum = sum_over_mp(sums("slh,srh->srl", cot_seq, u_out), n_mp)
        back_low = back_sum.astype(jnp.bfloat16)

        wide_in = hidden_full.astype(jnp.float32)
        mean_row = jnp.mean(wide_in, axis=-1, keepdims=True)
        centred = wide_in - mean_row
        inv_std = lax.rsqrt(jnp.mean(centred * centred, axis=-1, keepdims=True) + EPSILON)
        normed = (centred * inv_std * ln_gain + ln_bias).astype(jnp.bfloat16)
        normed_seq = by_seq(normed)
        low = sums("slm,srm->srl", normed_seq, a_in).astype(jnp.bfloat16)
        qkv_pre = (
            dot(normed, wide_qkv)
            + b_qkv.reshape(-1).astype(jnp.float32)
            + sums("srl,srh->slh", low[:, : 3 * rank], u_block).reshape(tokens, 3 * head_cols)
        )
        heads = head_cols // HEAD_DIM
        queries = (
            turned(qkv_pre[:, :head_cols], table, heads) * HEAD_DIM ** (-0.5)
        ).astype(jnp.bfloat16)
        keys = turned(qkv_pre[:, head_cols : 2 * head_cols], table, heads).astype(jnp.bfloat16)
        values = qkv_pre[:, 2 * head_cols :].astype(jnp.bfloat16)
        context, logs = attention(doc, queries, keys, values)

        grad_context = (
            lax.dot_general(
                cot_full, wide_out, (((1,), (1,)), ((), ())), preferred_element_type=SUMMATION_DTYPE
            )
            + sums("srl,srh->slh", back_low[:, :rank], a_o).reshape(tokens, head_cols)
        ).astype(jnp.bfloat16)
        grad_q, grad_k, grad_v = attention_back(
            doc, queries, keys, values, grad_context, logs, table
        )
        grad_qkv = jnp.concatenate([grad_q, grad_k, grad_v], axis=1)

        fc1_pre = (
            dot(normed, wide_fc1)
            + b_fc1.astype(jnp.float32)
            + sums("srl,srf->slf", low[:, 3 * rank :], u_fc1).reshape(tokens, ff_cols)
        )
        activated = gelu_tanh(fc1_pre).astype(jnp.bfloat16)
        slope = gelu_slope(fc1_pre).astype(jnp.bfloat16)
        grad_active = lax.dot_general(
            cot_full, wide_fc2, (((1,), (1,)), ((), ())), preferred_element_type=SUMMATION_DTYPE
        ) + sums("srl,srf->slf", back_low[:, rank:], a_fc2).reshape(tokens, ff_cols)
        grad_fc1 = (grad_active * slope.astype(jnp.float32)).astype(jnp.bfloat16)

        branch_sum = sum_over_mp(
            jnp.concatenate(
                [
                    sums("slh,srh->srl", by_seq(context), a_o),
                    sums("slf,srf->srl", by_seq(activated), a_fc2),
                ],
                axis=1,
            ),
            n_mp,
        )
        branch_low = branch_sum.astype(jnp.bfloat16)
        mixed = share_out(dot(context, wide_out) + dot(activated, wide_fc2), n_mp)
        output = (
            hidden_in.astype(jnp.float32)
            + mixed
            + b_out.astype(jnp.float32)
            + b_fc2.astype(jnp.float32)
            + sums("srl,srk->slk", branch_low, u_out).reshape(tokens, width)
        ).astype(jnp.bfloat16)

        rank_sum = sum_over_mp(
            jnp.concatenate(
                [
                    sums("slh,srh->srl", by_seq(grad_qkv), u_block),
                    sums("slf,srf->srl", by_seq(grad_fc1), u_fc1),
                ],
                axis=1,
            ),
            n_mp,
        )
        rank_low = rank_sum.astype(jnp.bfloat16)

        partial = lax.dot_general(
            grad_qkv, wide_qkv, (((1,), (1,)), ((), ())), preferred_element_type=SUMMATION_DTYPE
        ) + lax.dot_general(
            grad_fc1, wide_fc1, (((1,), (1,)), ((), ())), preferred_element_type=SUMMATION_DTYPE
        )
        a_mine = lax.dynamic_slice_in_dim(a_in, me * width, width, axis=2)
        gain = lax.dynamic_slice_in_dim(ln_gain, me * width, width)
        grad_normed = share_out(partial, n_mp) + sums("srl,srk->slk", rank_low, a_mine).reshape(
            tokens, width
        )
        scaled = grad_normed * gain
        x_hat = (hidden_in.astype(jnp.float32) - mean_row) * inv_std
        row_sums = sum_over_mp(
            jnp.stack([jnp.sum(scaled, axis=1), jnp.sum(scaled * x_hat, axis=1)]), n_mp
        ) / MODEL_WIDTH
        grad_in = (
            cotangent.astype(jnp.float32)
            + inv_std * (scaled - row_sums[0][:, None] - x_hat * row_sums[1][:, None])
        ).astype(jnp.bfloat16)

        share = 4 * rank // n_mp
        rank_mine = lax.dynamic_slice_in_dim(rank_low, me * share, share, axis=1)
        g_in = sums("srl,slm->srm", rank_mine, normed_seq)
        g_qkv = jnp.stack(
            [
                sums("srl,slh->srh", low[:, j * rank : (j + 1) * rank], by_seq(g))
                for j, g in enumerate((grad_q, grad_k, grad_v))
            ],
            axis=2,
        )
        g_fc1 = sums("srl,slf->srf", low[:, 3 * rank :], by_seq(grad_fc1))
        g_o = sums("srl,slh->srh", back_low[:, :rank], by_seq(context))
        g_fc2 = sums("srl,slf->srf", back_low[:, rank:], by_seq(activated))
        g_out = sums("srl,slk->srk", branch_low, cot_seq)
        sends = [
            jnp.moveaxis(g_in.reshape(seqs, share, n_dp, features), 2, 0),
            jnp.moveaxis(g_qkv.reshape(seqs, n_dp, ranks, 3, head_cols), 1, 0),
            jnp.moveaxis(g_fc1.reshape(seqs, n_dp, ranks, ff_cols), 1, 0),
            jnp.moveaxis(g_o.reshape(seqs, n_dp, ranks, head_cols), 1, 0),
            jnp.moveaxis(g_fc2.reshape(seqs, n_dp, ranks, ff_cols), 1, 0),
            jnp.moveaxis(g_out.reshape(seqs, 2, n_dp, ranks, width), 2, 0),
        ]
        shapes = [s.shape[2:] for s in sends]
        for_peer = jnp.concatenate(
            [s.reshape(n_dp, seqs, -1) for s in sends], axis=2
        ).astype(jnp.bfloat16)
        here = lax.axis_index("dp")
        arrived = []
        for k in range(n_dp):
            piece = lax.dynamic_index_in_dim(
                for_peer, lax.rem(here + k, n_dp), 0, keepdims=False
            )
            arrived.append(shift_dp(piece, n_dp, k) if k else piece)
        owned = lax.dot_general(
            one_hot(jnp.concatenate(ids)),
            jnp.concatenate(arrived, axis=0),
            (((0,), (0,)), ((), ())),
            preferred_element_type=SUMMATION_DTYPE,
        )
        outs, spot = [], 0
        for shape in shapes:
            size = 1
            for n in shape:
                size *= n
            outs.append(owned[:, spot : spot + size].reshape((NAD,) + shape))
            spot += size
        grad_down_x = lay_out(pieces_of(outs[0], n_mp), 1).reshape(NAD, 4, rank, features)
        return (output, grad_in, grad_down_x, *outs[1:])

    return body


def solution(mesh):
    in_specs = (
        P("dp", "mp"),
        P("dp", "mp"),
        P("dp", None),
        P("dp"),
        P(),
        P(),
        P("dp", None, "mp"),
        P(None, "mp"),
        P("mp", "dp"),
        P("mp"),
        P("dp", "mp"),
        P("mp"),
        P("mp", "dp"),
        P("mp"),
        P(None, None, None, "dp"),
        P(None, "dp", None, "mp"),
        P(None, "dp", "mp"),
        P(None, "dp", "mp"),
        P(None, "dp", "mp"),
        P(None, None, "dp", "mp"),
    )
    out_specs = (
        P("dp", "mp"),
        P("dp", "mp"),
        P(None, None, None, "dp"),
        P(None, "dp", None, "mp"),
        P(None, "dp", "mp"),
        P(None, "dp", "mp"),
        P(None, "dp", "mp"),
        P(None, None, "dp", "mp"),
    )
    return jax.shard_map(
        make_body(mesh.shape["dp"], mesh.shape["mp"]), mesh=mesh, in_specs=in_specs, out_specs=out_specs, check_vma=False)
```

time: 1510 us -> 952 us (0.63)
  waiting for transfers between devices: 560 us -> 163 us
  matrix products: 477 us -> 254 us
  blocking collectives: 203 us -> 0 us
  local copies, waits for them, and re-layouts: 89.5 us -> 231 us
  starting transfers between devices: 0.6 us -> 112 us
  other arithmetic: 156 us -> 78.2 us
  Pallas kernels: 0 us -> 73.3 us
    psum x1 -> x0, waiting for transfers between devices: 288 us -> none  [body(): normed_sum, rank_sum = lax.psum((normed_part, rank_part), 'mp')]
    reduce_scatter x6 -> x0, waiting for transfers between devices: 268 us -> none  [the longest x1 91.8 us: body(): lax.psum_scatter(partial_rows, 'mp', scatter_dimension=1, tiled=True)]
    dot_general x52 -> x30, matrix products: 477 us -> 254 us  [the longest x5 95.4 us: dot(): return jnp.dot(left, right, preferred_element_type=SUMMATION_DTYPE)]
    all_gather x5 -> x0, blocking collectives: 163 us -> none  [the longest x1 34.8 us: body(): lax.all_gather(down_fc2, 'dp', axis=1, tiled=True)]
    ppermute x0 -> x70, waiting for transfers between devices: none -> 163 us  [the longest x21 64.3 us: swap(): return lax.ppermute(value, axis, [(i, i ^ bit) for i in range(count)])]
    ppermute x0 -> x70, starting transfers between devices: none -> 112 us  [the longest x21 51.5 us: shift_dp(): lax.ppermute(value, 'dp', [(i, (i + shift) % count) for i in range(count)])]
    pallas_call x0 -> x2, Pallas kernels: none -> 73.3 us  [the longest x1 40.4 us: attention_back(): pl.pallas_call(attend_back_kernel, grid=(seq_count, pairs), in_specs=[doc...]
    concatenate x0 -> x12, local copies, waits for them, and re-layouts: none -> 66.5 us  [the longest x3 50.4 us: turned(): jnp.concatenate([t] * (heads * HEAD_DIM // PAIR), axis=1)]
  transfers between devices with their start and end apart: 15 -> 72, of which waited for: 5 -> 30; matrix products, arithmetic and copies ran while one was open for 47% -> 52% of each run, Pallas kernels for 0% -> 8%
where the time goes in v1:
time: 952 us; the launch traced here: 939 us
  matrix products  254 us (27%)
  local copies, waits for them, and re-layouts  231 us (24%)
  waiting for transfers between devices  163 us (17%)
  starting transfers between devices  112 us (12%)
  other arithmetic  78.2 us (8%)
  Pallas kernels  73.3 us (8%)
  between operations  27.4 us (3%)
    dot_general x5, matrix products, dot(): return jnp.dot(left, right, preferred_element_type=SUMMATION_DTYPE)  95.4 us
    ppermute x21, waiting for transfers between devices, swap(): return lax.ppermute(value, axis, [(i, i ^ bit) for i in range(count)])  64.3 us
    dot_general x20, matrix products, sums(): return jnp.einsum(spec, left, right, preferred_element_type=SUMMATION_DTYPE)  64.2 us
    ppermute x28, waiting for transfers between devices, ring_gather(): moving = lax.ppermute(moving, 'dp', route)  52.9 us
    ppermute x21, starting transfers between devices, shift_dp(): lax.ppermute(value, 'dp', [(i, (i + shift) % count) for i in range(count)])  51.5 us
    concatenate x3, local copies, waits for them, and re-layouts, turned(): jnp.concatenate([t] * (heads * HEAD_DIM // PAIR), axis=1)  50.4 us
    ppermute x28, starting transfers between devices, ring_gather(): moving = lax.ppermute(moving, 'dp', route)  49 us
    ppermute x21, waiting for transfers between devices, shift_dp(): lax.ppermute(value, 'dp', [(i, (i + shift) % count) for i in range(count)])  45.4 us
  transfers between devices with their start and end apart: 72, of which 30 were waited for; matrix products, arithmetic and copies ran while one was open for 52% of the time, Pallas kernels for 8%

profile of v1, /device:TPU:0, one launch (start us, length us, event | category | flops | bytes accessed | tf_op | source)
XLA Modules:
  0.0 939.3 jit_solution(18434962693097472433)
XLA Ops:
  37.5 17.0 %concatenate.90 = f32[2048,512]{1,0:T(8,128)} concatenate(f32[2048,16]{1,0:T(8,128)S(1)} %get-tuple-element.81, f32[2048,16]{1,0:T(8,128)S(1)} %broadcast_in_dim.54, f32[2048,32]{1,0:T(8,128)} %broadcast_in_dim.55, f32[2048,16]{1,0:T(8,128)S(1)} %get-tuple-element.81, f32[2048,16]{1,0:T(8,128)S(1)} %broadcast_in_dim.54, f32[2048,32]{1,0:T(8,128)} %broadcast_in_dim.55, ...), dimensions={1} | concatenate | bytes 8388608 | tf_op jit(solution)/shard_map/concatenate | solution.py:320
  54.6 17.0 %concatenate.92 = f32[2048,512]{1,0:T(8,128)} concatenate(f32[2048,16]{1,0:T(8,128)S(1)} %broadcast_in_dim.54, f32[2048,16]{1,0:T(8,128)S(1)} %get-tuple-element.81, f32[2048,32]{1,0:T(8,128)} %broadcast_in_dim.55, f32[2048,16]{1,0:T(8,128)S(1)} %broadcast_in_dim.54, f32[2048,16]{1,0:T(8,128)S(1)} %get-tuple-element.81, f32[2048,32]{1,0:T(8,128)} %broadcast_in_dim.55, ...), dimensions={1} | concatenate | bytes 8388608 | tf_op jit(solution)/shard_map/concatenate | solution.py:320
  81.3 16.3 %concatenate.88 = f32[2048,512]{1,0:T(8,128)} concatenate(f32[2048,16]{1,0:T(8,128)S(1)} %get-tuple-element.82, f32[2048,16]{1,0:T(8,128)S(1)} %get-tuple-element.82, f32[2048,32]{1,0:T(8,128)S(1)} %broadcast_in_dim.53, f32[2048,16]{1,0:T(8,128)S(1)} %get-tuple-element.82, f32[2048,16]{1,0:T(8,128)S(1)} %get-tuple-element.82, f32[2048,32]{1,0:T(8,128)S(1)} %broadcast_in_dim.53, ...), dimensions={1} | concatenate | bytes 8388608 | tf_op jit(solution)/shard_map/concatenate | solution.py:320
  170.4 8.1 collective-permute-start.27
  192.4 8.5 collective-permute-done.28
  271.2 9.6 %collective-permute-start.39 = (bf16[256,256]{1,0:T(8,128)(2,1)S(1)}, bf16[256,256]{1,0:T(8,128)(2,1)S(1)}, u32[]{:S(2)}, u32[]{:S(2)}) collective-permute-start(bf16[256,256]{1,0:T(8,128)(2,1)S(1)} %collective-permute-done.35), channel_id=1, source_target_pairs={{0,8},{8,16},{16,24},{24,28},{28,20},{20,12},{12,4},{4,0},{1,9},{9... | collective-permute-start | bytes 393224 | tf_op jit(solution)/shard_map/ppermute | solution.py:226
  330.1 8.2 fusion.55
  379.6 9.6 %collective-permute-done.50 = bf16[2048,512]{1,0:T(8,128)(2,1)} collective-permute-done((bf16[2048,512]{1,0:T(8,128)(2,1)S(1)}, bf16[2048,512]{1,0:T(8,128)(2,1)}, u32[]{:S(2)}, u32[]{:S(2)}) %collective-permute-start.50) | collective-permute-done | bytes 2097184 | tf_op jit(solution)/shard_map/ppermute | solution.py:238
  414.2 22.1 %bitcast_add_fusion.2 = f32[2048,1536]{1,0:T(8,128)} fusion(f32[2,1024,1536]{2,1,0:T(8,128)} %fusion.46, bf16[2048,2048]{1,0:T(8,128)(2,1)} %copy-done, bf16[2048,1536]{0,1:T(8,128)(2,1)} %constant_dynamic-update-slice_fusion.30, f32[1536]{0:T(1024)S(1)} %reshape.473), kind=kOutput, calls=%fused_computation.24 | convolution fusion | flops 12891193344 | bytes 39852032 | tf_op jit(solution)/shard_map/dot_general | solution.py:298
  463.1 15.7 %fusion.30 = (bf16[2048,512]{1,0:T(8,128)(2,1)}, bf16[2048,512]{1,0:T(8,128)(2,1)}) fusion(f32[2048,512]{1,0:T(8,128)} %concatenate.88, f32[2048,1536]{1,0:T(8,128)} %bitcast_add_fusion.2, f32[2048,512]{1,0:T(8,128)S(1)} %copy-done.10, f32[2048,16]{1,0:T(8,128)S(1)} %get-tuple-element.42, f32[2048,496]{1,0:T(8,128)} %get-tuple-element.46, ...), kind=kLoop, calls=%fused_computation.51 | loop fusion | flops 17825792 | bytes 41943040 | tf_op jit(solution)/shard_map/convert_element_type | solution.py:402
  478.8 32.8 %attend.1 = (bf16[2048,512]{1,0:T(8,128)(2,1)}, f32[2,4,2,1024]{3,2,1,0:T(2,128)}) custom-call(s32[2,1,1024]{2,1,0:T(1,128)} %bitcast.323, bf16[2048,512]{1,0:T(8,128)(2,1)} %get-tuple-element.40.q_ref, bf16[2048,512]{1,0:T(8,128)(2,1)} %get-tuple-element.39.k_ref, bf16[2048,512]{1,0:T(8,128)(2,1)} %slice.324.v_ref), custom_call_target="tpu_custom_call" | custom-call | flops 4831838208 | bytes 8388608 | tf_op jit(solution)/shard_map/attend/pallas_call | solution.py:153
  511.6 11.1 %fusion.37.g_ref = bf16[2048,512]{1,0:T(8,128)(2,1)} fusion(f32[2,1024,512]{2,1,0:T(8,128)} %fusion.58, bf16[2048,2048]{1,0:T(8,128)(2,1)} %copy-done.12, bf16[512,2048]{1,0:T(8,128)(2,1)} %constant_dynamic-update-slice_fusion.50), kind=kOutput, calls=%fused_computation.65 | convolution fusion | flops 4297064448 | bytes 16777216 | tf_op jit(solution)/shard_map/dot_general | solution.py:407
  522.8 40.4 %attend_back.1 = (bf16[2048,512]{1,0:T(8,128)(2,1)}, bf16[2048,512]{1,0:T(8,128)(2,1)}, bf16[2048,512]{1,0:T(8,128)(2,1)}) custom-call(s32[2,1,1024]{2,1,0:T(1,128)} %bitcast.324, bf16[2048,512]{1,0:T(8,128)(2,1)} %get-tuple-element.40.q_ref, bf16[2048,512]{1,0:T(8,128)(2,1)} %get-tuple-element.39.k_ref, bf16[2048,512]{1,0:T(8,128)(2,1)} %slice.324.v_ref, ...), custom_call_target="tpu_custom_call" | custom-call | flops 12079595520 | bytes 14680064 | tf_op jit(solution)/shard_map/attend_back/pallas_call | solution.py:174
  577.3 8.2 fusion.61
  585.5 31.3 %fusion.13 = (bf16[2048,2048]{1,0:T(8,128)(2,1)}, f32[2048,2048]{1,0:T(8,128)}) fusion(f32[2,1024,2048]{2,1,0:T(8,128)} %fusion.61, f32[2048]{0:T(1024)S(1)} %copy-done.50, bf16[2048,2048]{1,0:T(8,128)(2,1)} %copy-done, bf16[2048,2048]{1,0:T(8,128)(2,1)} %all-gather.3.cloned.1.call-done), kind=kOutput, calls=%fused_computation.18 | convolution fusion | flops 17226006528 | bytes 58728448 | tf_op jit(solution)/shard_map/dot_general | solution.py:298
  616.8 36.9 %fusion.15 = bf16[2048,2048]{1,0:T(8,128)(2,1)} fusion(f32[2,1024,2048]{2,1,0:T(8,128)} %fusion.55, bf16[2048,2048]{1,0:T(8,128)(2,1)} %copy-done.12, bf16[2048,2048]{1,0:T(8,128)(2,1)} %all-gather.5.cloned.1.call-done, f32[2048,2048]{1,0:T(8,128)} %get-tuple-element.93), kind=kOutput, calls=%fused_computation.21 | convolution fusion | flops 17267949568 | bytes 58720256 | tf_op jit(solution)/shard_map/dot_general | solution.py:424
  668.6 23.2 %fusion.87 = f32[2048,2048]{0,1:T(8,128)} fusion(bf16[2048,2048]{1,0:T(8,128)(2,1)S(1)} %bitcast.249, bf16[2048,2048]{1,0:T(8,128)(2,1)} %all-gather.5.cloned.1.call-done), kind=kOutput, calls=%fused_computation.249 | convolution fusion | flops 17179869184 | bytes 33554432 | tf_op jit(solution)/shard_map/dot_general | solution.py:298
  691.7 17.4 %convolution_add_fusion.1 = f32[2048,2048]{0,1:T(8,128)} fusion(f32[2048,2048]{0,1:T(8,128)} %fusion.87, bf16[2048,512]{1,0:T(8,128)(2,1)} %get-tuple-element.13, bf16[512,2048]{1,0:T(8,128)(2,1)} %constant_dynamic-update-slice_fusion.50), kind=kOutput, calls=%fused_computation.32 | convolution fusion | flops 4299161600 | bytes 37748736 | tf_op jit(solution)/shard_map/dot_general | solution.py:298
  709.1 24.4 %fusion.92 = f32[2048,2048]{0,1:T(8,128)} fusion(bf16[2048,2048]{1,0:T(8,128)(2,1)} %fusion.15, bf16[2048,2048]{1,0:T(8,128)(2,1)} %all-gather.3.cloned.1.call-done), kind=kOutput, calls=%fused_computation.254 | convolution fusion | flops 17179869184 | bytes 33554432 | tf_op jit(solution)/shard_map/dot_general | solution.py:463
  733.5 21.8 %convolution_add_fusion = f32[2048,2048]{0,1:T(8,128)} fusion(f32[2048,2048]{0,1:T(8,128)} %fusion.92, bf16[2048,1536]{1,0:T(8,128)(2,1)} %copy-done.11, bf16[2048,1536]{0,1:T(8,128)(2,1)} %constant_dynamic-update-slice_fusion.30), kind=kOutput, calls=%fused_computation.25 | convolution fusion | flops 12889096192 | bytes 46137344 | tf_op jit(solution)/shard_map/dot_general | solution.py:461
  769.6 8.7 collective-permute-done.57
  849.8 10.2 %bitcast_add_fusion.4 = f32[2048,1024]{0,1:T(8,128)} fusion(f32[2048,2,1,512]{0,3,2,1:T(8,128)} %constant_dynamic-slice_fusion.6, bf16[2048,1024]{0,1:T(8,128)(2,1)} %collective-permute-done.45), kind=kLoop, calls=%fused_computation.29 | loop fusion | flops 4194304 | bytes 20971520 | tf_op jit(solution)/shard_map/add | solution.py:279
  864.4 11.2 %collective-permute-done.55 = bf16[2048,512]{0,1:T(8,128)(2,1)} collective-permute-done((bf16[2048,512]{0,1:T(8,128)(2,1)}, bf16[2048,512]{0,1:T(8,128)(2,1)}, u32[]{:S(2)}, u32[]{:S(2)}) %collective-permute-start.55) | collective-permute-done | bytes 2097184 | tf_op jit(solution)/shard_map/ppermute | solution.py:238
  885.0 33.6 %collective-permute-done.59 = f32[2,2048]{1,0:T(2,128)S(1)} collective-permute-done((f32[2,2048]{1,0:T(2,128)S(1)}, f32[2,2048]{1,0:T(2,128)S(1)}, u32[]{:S(2)}, u32[]{:S(2)}) %collective-permute-start.59) | collective-permute-done | bytes 16416 | tf_op jit(solution)/shard_map/ppermute | solution.py:238
  (492 shorter events, 468.4 us)
Async XLA Ops:
  7.2 578.3 %all-gather.3.cloned.1.call-start = ((), (), s32[]{:S(2)}) async-start(), calls=%async_computation | async-start | bytes 9437184 | tf_op jit(solution)/shard_map/all_gather | solution.py:373
  7.9 608.9 %all-gather.5.cloned.1.call-start = ((), (), s32[]{:S(2)}) async-start(), calls=%async_computation.1 | async-start | bytes 9437184 | tf_op jit(solution)/shard_map/all_gather | solution.py:374
  7.9 336.8 %collective-permute-start.1 = (bf16[2048,512]{1,0:T(8,128)(2,1)}, bf16[2048,512]{1,0:T(8,128)(2,1)}, u32[]{:S(2)}, u32[]{:S(2)}) collective-permute-start(bf16[2048,512]{1,0:T(8,128)(2,1)} %param.24), channel_id=1, source_target_pairs={{0,2},{1,3},{2,0},{3,1},{4,6},{5,7},{6,4},{7,5},{8,10},{9,11},{10,... | collective-permute-start | bytes 6291464 | tf_op jit(solution)/shard_map/ppermute | solution.py:238
  11.0 378.2 %collective-permute-start = (bf16[2048,512]{1,0:T(8,128)(2,1)}, bf16[2048,512]{1,0:T(8,128)(2,1)}, u32[]{:S(2)}, u32[]{:S(2)}) collective-permute-start(bf16[2048,512]{1,0:T(8,128)(2,1)} %param.24), channel_id=1, source_target_pairs={{0,1},{1,0},{2,3},{3,2},{4,5},{5,4},{6,7},{7,6},{8,9},{9,8},{10,11... | collective-permute-start | bytes 6291464 | tf_op jit(solution)/shard_map/ppermute | solution.py:238
  11.0 117.2 %collective-permute-start.17 = (s32[2]{0:T(128)}, s32[2]{0:T(128)}, u32[]{:S(2)}, u32[]{:S(2)}) collective-permute-start(s32[2]{0:T(128)} %param.27), channel_id=1, source_target_pairs={{0,28},{4,0},{8,4},{12,8},{16,12},{20,16},{24,20},{28,24},{1,29},{... | collective-permute-start | bytes 32 | tf_op jit(solution)/shard_map/ppermute | solution.py:284
  15.5 115.6 %collective-permute-start.18 = (s32[2]{0:T(128)}, s32[2]{0:T(128)}, u32[]{:S(2)}, u32[]{:S(2)}) collective-permute-start(s32[2]{0:T(128)} %param.27), channel_id=1, source_target_pairs={{0,24},{4,28},{8,0},{12,4},{16,8},{20,12},{24,16},{28,20},{1,25},{... | collective-permute-start | bytes 32 | tf_op jit(solution)/shard_map/ppermute | solution.py:284
  16.0 115.2 %collective-permute-start.19 = (s32[2]{0:T(128)}, s32[2]{0:T(128)}, u32[]{:S(2)}, u32[]{:S(2)}) collective-permute-start(s32[2]{0:T(128)} %param.27), channel_id=1, source_target_pairs={{0,20},{4,24},{8,28},{12,0},{16,4},{20,8},{24,12},{28,16},{1,21},{... | collective-permute-start | bytes 32 | tf_op jit(solution)/shard_map/ppermute | solution.py:284
  136.6 107.8 %collective-permute-start.31 = (bf16[256,256]{1,0:T(8,128)(2,1)}, bf16[256,256]{1,0:T(8,128)(2,1)}, u32[]{:S(2)}, u32[]{:S(2)}) collective-permute-start(bf16[256,256]{1,0:T(8,128)(2,1)} %get-tuple-element.75), channel_id=1, source_target_pairs={{0,8},{8,16},{16,24},{24,28},{28,20},{20,12},{12,4},{4,0},{1,9},{9... | collective-permute-start | bytes 393224 | tf_op jit(solution)/shard_map/ppermute | solution.py:226
  137.5 109.2 %collective-permute-start.32 = (bf16[256,256]{1,0:T(8,128)(2,1)}, bf16[256,256]{1,0:T(8,128)(2,1)}, u32[]{:S(2)}, u32[]{:S(2)}) collective-permute-start(bf16[256,256]{1,0:T(8,128)(2,1)} %get-tuple-element.75), channel_id=1, source_target_pairs={{8,0},{16,8},{24,16},{28,24},{20,28},{12,20},{4,12},{0,4},{9,1},{1... | collective-permute-start | bytes 393224 | tf_op jit(solution)/shard_map/ppermute | solution.py:226
  220.2 28.0 %collective-permute-start.33 = (bf16[256,256]{1,0:T(8,128)(2,1)}, bf16[256,256]{1,0:T(8,128)(2,1)}, u32[]{:S(2)}, u32[]{:S(2)}) collective-permute-start(bf16[256,256]{1,0:T(8,128)(2,1)} %get-tuple-element.73), channel_id=1, source_target_pairs={{0,8},{8,16},{16,24},{24,28},{28,20},{20,12},{12,4},{4,0},{1,9},{9... | collective-permute-start | bytes 393224 | tf_op jit(solution)/shard_map/ppermute | solution.py:226
  246.7 38.5 %collective-permute-start.52 = (f32[2,32,1024]{2,1,0:T(8,128)}, f32[2,32,1024]{2,1,0:T(8,128)S(1)}, u32[]{:S(2)}, u32[]{:S(2)}) collective-permute-start(f32[2,32,1024]{2,1,0:T(8,128)} %fusion.91), channel_id=1, source_target_pairs={{0,1},{1,0},{2,3},{3,2},{4,5},{5,4},{6,7},{7,6},{8,9},{9,8},{10,11... | collective-permute-start | bytes 786440 | tf_op jit(solution)/shard_map/ppermute | solution.py:238
  285.1 21.0 %collective-permute-start.3 = (bf16[128,1536]{0,1:T(8,128)(2,1)S(1)}, bf16[128,1536]{0,1:T(8,128)(2,1)S(1)}, u32[]{:S(2)}, u32[]{:S(2)}) collective-permute-start(bf16[128,1536]{0,1:T(8,128)(2,1)S(1)} %bitcast.281), channel_id=1, source_target_pairs={{0,8},{8,16},{16,24},{24,28},{28,20},{20,12},{12,4},{4,0},{1,9},{9... | collective-permute-start | bytes 1179656 | tf_op jit(solution)/shard_map/ppermute | solution.py:226
  344.3 44.9 %collective-permute-start.50 = (bf16[2048,512]{1,0:T(8,128)(2,1)S(1)}, bf16[2048,512]{1,0:T(8,128)(2,1)}, u32[]{:S(2)}, u32[]{:S(2)}) collective-permute-start(bf16[2048,512]{1,0:T(8,128)(2,1)S(1)} %copy-done.2), channel_id=1, source_target_pairs={{0,2},{1,3},{2,0},{3,1},{4,6},{5,7},{6,4},{7,5},{8,10},{9,11},{10,... | collective-permute-start | bytes 6291464 | tf_op jit(solution)/shard_map/ppermute | solution.py:238
  344.8 44.4 %collective-permute-start.2 = (bf16[2048,512]{1,0:T(8,128)(2,1)}, bf16[2048,512]{1,0:T(8,128)(2,1)S(1)}, u32[]{:S(2)}, u32[]{:S(2)}) collective-permute-start(bf16[2048,512]{1,0:T(8,128)(2,1)} %collective-permute-done.1), channel_id=1, source_target_pairs={{0,1},{1,0},{2,3},{3,2},{4,5},{5,4},{6,7},{7,6},{8,9},{9,8},{10,11... | collective-permute-start | bytes 6291464 | tf_op jit(solution)/shard_map/ppermute | solution.py:238
  377.9 58.4 %collective-permute-start.49 = (bf16[2048,512]{1,0:T(8,128)(2,1)S(1)}, bf16[2048,512]{1,0:T(8,128)(2,1)}, u32[]{:S(2)}, u32[]{:S(2)}) collective-permute-start(bf16[2048,512]{1,0:T(8,128)(2,1)S(1)} %copy-done.2), channel_id=1, source_target_pairs={{0,1},{1,0},{2,3},{3,2},{4,5},{5,4},{6,7},{7,6},{8,9},{9,8},{10,11... | collective-permute-start | bytes 6291464 | tf_op jit(solution)/shard_map/ppermute | solution.py:238
  389.2 47.1 %collective-permute-start.51 = (bf16[2048,512]{1,0:T(8,128)(2,1)}, bf16[2048,512]{1,0:T(8,128)(2,1)}, u32[]{:S(2)}, u32[]{:S(2)}) collective-permute-start(bf16[2048,512]{1,0:T(8,128)(2,1)} %collective-permute-done.50), channel_id=1, source_target_pairs={{0,1},{1,0},{2,3},{3,2},{4,5},{5,4},{6,7},{7,6},{8,9},{9,8},{10,11... | collective-permute-start | bytes 6291464 | tf_op jit(solution)/shard_map/ppermute | solution.py:238
  665.0 93.6 %collective-permute-start.56 = (f32[2,64,1024]{2,1,0:T(8,128)}, f32[2,64,1024]{2,1,0:T(8,128)}, u32[]{:S(2)}, u32[]{:S(2)}) collective-permute-start(f32[2,64,1024]{2,1,0:T(8,128)} %pad_maximum_fusion.3), channel_id=1, source_target_pairs={{0,1},{1,0},{2,3},{3,2},{4,5},{5,4},{6,7},{7,6},{8,9},{9,8},{10,11... | collective-permute-start | bytes 1572872 | tf_op jit(solution)/shard_map/ppermute | solution.py:238
  668.5 87.9 %collective-permute-start.47 = (f32[2,32,1024]{2,1,0:T(8,128)}, f32[2,32,1024]{2,1,0:T(8,128)}, u32[]{:S(2)}, u32[]{:S(2)}) collective-permute-start(f32[2,32,1024]{2,1,0:T(8,128)} %pad_maximum_fusion.5), channel_id=1, source_target_pairs={{0,1},{1,0},{2,3},{3,2},{4,5},{5,4},{6,7},{7,6},{8,9},{9,8},{10,11... | collective-permute-start | bytes 786440 | tf_op jit(solution)/shard_map/ppermute | solution.py:238
  759.7 18.6 %collective-permute-start.57 = (f32[2,64,1024]{2,1,0:T(8,128)S(1)}, f32[2,64,1024]{2,1,0:T(8,128)}, u32[]{:S(2)}, u32[]{:S(2)}) collective-permute-start(f32[2,64,1024]{2,1,0:T(8,128)S(1)} %fusion.75), channel_id=1, source_target_pairs={{0,2},{1,3},{2,0},{3,1},{4,6},{5,7},{6,4},{7,5},{8,10},{9,11},{10,... | collective-permute-start | bytes 1572872 | tf_op jit(solution)/shard_map/ppermute | solution.py:238
  767.9 51.1 %collective-permute-start.54 = (bf16[2048,1024]{0,1:T(8,128)(2,1)}, bf16[2048,1024]{0,1:T(8,128)(2,1)}, u32[]{:S(2)}, u32[]{:S(2)}) collective-permute-start(bf16[2048,1024]{0,1:T(8,128)(2,1)} %bitcast.272), channel_id=1, source_target_pairs={{0,1},{1,0},{2,3},{3,2},{4,5},{5,4},{6,7},{7,6},{8,9},{9,8},{10,11... | collective-permute-start | bytes 12582920 | tf_op jit(solution)/shard_map/ppermute | solution.py:238
  791.7 58.0 %collective-permute-start.45 = (bf16[2048,1024]{0,1:T(8,128)(2,1)}, bf16[2048,1024]{0,1:T(8,128)(2,1)}, u32[]{:S(2)}, u32[]{:S(2)}) collective-permute-start(bf16[2048,1024]{0,1:T(8,128)(2,1)} %bitcast.45), channel_id=1, source_target_pairs={{0,1},{1,0},{2,3},{3,2},{4,5},{5,4},{6,7},{7,6},{8,9},{9,8},{10,11... | collective-permute-start | bytes 12582920 | tf_op jit(solution)/shard_map/ppermute | solution.py:238
  826.7 48.8 %collective-permute-start.55 = (bf16[2048,512]{0,1:T(8,128)(2,1)}, bf16[2048,512]{0,1:T(8,128)(2,1)}, u32[]{:S(2)}, u32[]{:S(2)}) collective-permute-start(bf16[2048,512]{0,1:T(8,128)(2,1)} %fusion.39), channel_id=1, source_target_pairs={{0,2},{1,3},{2,0},{3,1},{4,6},{5,7},{6,4},{7,5},{8,10},{9,11},{10,... | collective-permute-start | bytes 6291464 | tf_op jit(solution)/shard_map/ppermute | solution.py:238
  863.9 54.8 %collective-permute-start.46 = (bf16[2048,512]{0,1:T(8,128)(2,1)}, bf16[2048,512]{0,1:T(8,128)(2,1)}, u32[]{:S(2)}, u32[]{:S(2)}) collective-permute-start(bf16[2048,512]{0,1:T(8,128)(2,1)} %fusion.38), channel_id=1, source_target_pairs={{0,2},{1,3},{2,0},{3,1},{4,6},{5,7},{6,4},{7,5},{8,10},{9,11},{10,... | collective-permute-start | bytes 6291464 | tf_op jit(solution)/shard_map/ppermute | solution.py:238
  882.4 36.2 %collective-permute-start.59 = (f32[2,2048]{1,0:T(2,128)S(1)}, f32[2,2048]{1,0:T(2,128)S(1)}, u32[]{:S(2)}, u32[]{:S(2)}) collective-permute-start(f32[2,2048]{1,0:T(2,128)S(1)} %fusion.70), channel_id=1, source_target_pairs={{0,2},{1,3},{2,0},{3,1},{4,6},{5,7},{6,4},{7,5},{8,10},{9,11},{10,... | collective-permute-start | bytes 49160 | tf_op jit(solution)/shard_map/ppermute | solution.py:238
  (110 other events, 1697.1 us)
Sparse Core Ops, SparseCore 0:
  10.1 127.2 all-gather.2
  139.4 150.5 all-gather.4
